TPU v7x, 256 devices: a whole 4x4x8 slice. The times are simulated.
256 devices in a mesh: section: 4 (over y), tm: 64 (over z, x, core).
Axes of the slice: x: 4, y: 4, z: 8, core: 2. Of those that a mesh axis runs over, the one named last changes fastest.
Arguments:
- inputs: bfloat16 [3, 8192, 1024], P(None, 'tm', 'section'), may hold values from -6 to 6
- lengths: int32 [3], replicated, may hold values from 2048 to 8192, as said below
- w_expand: bfloat16 [2, 4, 1024, 2048], P(None, 'section'), may hold values from -0.1875 to 0.1875
- w_project: bfloat16 [2, 4, 1024, 1024], P(None, 'section'), may hold values from -0.1875 to 0.1875
- kernel: float32 [2, 4, 32, 1024], P(None, 'section'), may hold values from -1.5 to 1.5
- gain: float32 [2, 4, 1024], P(None, 'section'), may hold values from 0.1 to 1.9
Outputs:
- encoded: bfloat16 [3, 8192, 1024], P(None, 'tm', 'section')
Inputs may be any that keep to these rules, and one draw needn't show every extreme that they name: lengths[0] is 8192.
All inputs are finite; a program needn't handle non-finite values.
Results may differ from a plain program's by a relative error of at most 0.022.
Values may be sent and summed in bfloat16 or wider, within the bound.
A program may use at most 64 MiB of HBM per device.

v0:
```python
import functools

import jax
import jax.numpy as jnp
from jax import lax
from jax.experimental import pallas as pl
from jax.experimental.pallas import tpu as pltpu
from jax.sharding import PartitionSpec as P

MESH = pl.DeviceIdType.MESH
ROWS = 32
HALO = 32
COLS = 256


def normalise(values):
    center = values - jnp.mean(values, axis=-1, keepdims=True)
    variance = jnp.mean(center * center, axis=-1, keepdims=True)
    return center * lax.rsqrt(variance + 1e-05)


def relay_kernel(
    sections,
    tms,
    lengths_ref,
    inputs_hbm,
    w_expand_hbm,
    w_project_hbm,
    kernel_hbm,
    gain_hbm,
    out_hbm,
    w1,
    w2,
    taps,
    gain,
    wide_taps,
    slots,
    outs,
    rims,
    tails,
    gated,
    depthwise,
    w_sems,
    small_sems,
    slot_send,
    slot_recv,
    rim_send,
    rim_recv,
    entry_send,
    entry_recv,
    exit_send,
    exit_recv,
):
    section = lax.axis_index("section")
    tm = lax.axis_index("tm")
    micro, frames, width = inputs_hbm.shape
    passes, feats, _ = w1.shape
    taps_len = taps.shape[1]
    chunks = frames // ROWS
    jobs = micro * passes
    last = sections - 1

    def weight_copies(pass_idx):
        return (
            pltpu.make_async_copy(w_expand_hbm.at[pass_idx], w1.at[pass_idx], w_sems.at[0, pass_idx]),
            pltpu.make_async_copy(w_project_hbm.at[pass_idx], w2.at[pass_idx], w_sems.at[1, pass_idx]),
        )

    taps_copy = pltpu.make_async_copy(kernel_hbm, taps, small_sems.at[0])
    gain_copy = pltpu.make_async_copy(gain_hbm, gain, small_sems.at[1])
    taps_copy.start()
    gain_copy.start()
    for copy in weight_copies(0):
        copy.start()
    for copy in weight_copies(1):
        copy.start()

    barrier = pltpu.get_barrier_semaphore()
    for step in range(1, sections):
        pl.semaphore_signal(
            barrier, inc=1, device_id={"section": (section + step) % sections}, device_id_type=MESH
        )

    @pl.when(tm > 0)
    def _():
        pl.semaphore_signal(barrier, inc=1, device_id={"tm": tm - 1}, device_id_type=MESH)

    @pl.when(tm < tms - 1)
    def _():
        pl.semaphore_signal(barrier, inc=1, device_id={"tm": tm + 1}, device_id_type=MESH)

    greeted = sections - 1 + (tm > 0).astype(jnp.int32) + (tm < tms - 1).astype(jnp.int32)
    pl.semaphore_wait(barrier, greeted)

    def entry_remote(m, source):
        return pltpu.make_async_remote_copy(
            src_ref=inputs_hbm.at[m],
            dst_ref=slots.at[m, :, pl.ds(pl.multiple_of(source * width, width), width)],
            send_sem=entry_send.at[m],
            recv_sem=entry_recv.at[m, source],
            device_id={"section": 0},
            device_id_type=MESH,
        )

    def entry_local(m):
        return pltpu.make_async_copy(
            inputs_hbm.at[m], slots.at[m, :, pl.ds(0, width)], entry_recv.at[m, 0]
        )

    @pl.when(section == 0)
    def _():
        for m in range(micro):
            entry_local(m).start()

    @pl.when(section != 0)
    def _():
        for m in range(micro):
            entry_remote(m, section).start()

    taps_copy.wait()
    gain_copy.wait()
    for pass_idx in range(passes):
        for k in range(taps_len):
            wide_taps[pass_idx, k] = jnp.broadcast_to(taps[pass_idx, k : k + 1, :], (8, feats))

    def slot_copy(job, chunk):
        slot = job + jnp.where(section == last, micro, 0)
        rows = pl.ds(pl.multiple_of(chunk * ROWS, ROWS), ROWS)
        return pltpu.make_async_remote_copy(
            src_ref=outs.at[job, rows],
            dst_ref=slots.at[slot, rows],
            send_sem=slot_send.at[job, chunk],
            recv_sem=slot_recv.at[slot, chunk],
            device_id={"section": (section + 1) % sections},
            device_id_type=MESH,
        )

    def slot_arrival(job, chunk):
        rows = pl.ds(pl.multiple_of(chunk * ROWS, ROWS), ROWS)
        return pltpu.make_async_remote_copy(
            src_ref=outs.at[job, rows],
            dst_ref=slots.at[job, rows],
            send_sem=slot_send.at[job, chunk],
            recv_sem=slot_recv.at[job, chunk],
            device_id={"section": (section + 1) % sections},
            device_id_type=MESH,
        )

    def rim_copy(job):
        return pltpu.make_async_remote_copy(
            src_ref=tails.at[job],
            dst_ref=rims.at[job],
            send_sem=rim_send.at[job],
            recv_sem=rim_recv.at[job],
            device_id={"tm": tm + 1},
            device_id_type=MESH,
        )

    def exit_remote(m, chunk, target):
        rows = pl.ds(pl.multiple_of(chunk * ROWS, ROWS), ROWS)
        return pltpu.make_async_remote_copy(
            src_ref=outs.at[m + (jobs - micro), rows, pl.ds(target * width, width)],
            dst_ref=out_hbm.at[m, rows],
            send_sem=exit_send.at[m, chunk, target],
            recv_sem=exit_recv.at[m, chunk],
            device_id={"section": target},
            device_id_type=MESH,
        )

    def exit_local(m, chunk):
        rows = pl.ds(pl.multiple_of(chunk * ROWS, ROWS), ROWS)
        return pltpu.make_async_copy(
            outs.at[m + (jobs - micro), rows, pl.ds(last * width, width)],
            out_hbm.at[m, rows],
            exit_recv.at[m, chunk],
        )

    def run_job(job, _):
        pass_idx = job // micro
        m = job % micro
        length = lengths_ref[m]
        first = jnp.logical_and(section == 0, pass_idx == 0)
        leaving = jnp.logical_and(section == last, pass_idx == passes - 1)

        def row_mask(chunk):
            rows = lax.broadcasted_iota(jnp.int32, (ROWS, 1), 0) + (tm * frames + chunk * ROWS)
            return rows < length

        @pl.when(first)
        def _():
            entry_local(m).wait()
            for source in range(1, sections):
                entry_remote(m, source).wait_recv()

        def expand(chunk):
            @pl.when(jnp.logical_not(first))
            def _():
                slot_arrival(job, chunk).wait_recv()

            if chunk == chunks - 1:

                @pl.when(m == 0)
                def _():
                    weight_copies(pass_idx)[0].wait()

            values = slots[job, chunk * ROWS : (chunk + 1) * ROWS, :].astype(jnp.float32)
            normed = (normalise(values) * gain[pass_idx]).astype(jnp.bfloat16)
            mask = row_mask(chunk)
            for block in range(feats // COLS):
                low = block * COLS
                value = jnp.dot(
                    normed, w1[pass_idx, :, low : low + COLS], preferred_element_type=jnp.float32
                )
                gate = jnp.dot(
                    normed,
                    w1[pass_idx, :, feats + low : feats + low + COLS],
                    preferred_element_type=jnp.float32,
                )
                passed = jnp.where(mask, value * jax.nn.sigmoid(gate), 0.0).astype(jnp.bfloat16)
                gated[HALO + chunk * ROWS : HALO + (chunk + 1) * ROWS, low : low + COLS] = (
                    passed.astype(jnp.float32)
                )
                if chunk == chunks - 1:
                    tails[job, :, low : low + COLS] = passed[ROWS - HALO :, :]
            if chunk == chunks - 1:

                @pl.when(tm < tms - 1)
                def _():
                    rim_copy(job).start()

        def finish(chunk):
            for block in range(feats // 128):
                cols = slice(block * 128, (block + 1) * 128)
                window = gated[chunk * ROWS : (chunk + 1) * ROWS + HALO, cols]
                total = jnp.zeros((ROWS // 8, 8, 128), jnp.float32)
                for back in range(8):
                    moved = window if back == 0 else pltpu.roll(window, back, 0)
                    tiles = moved.reshape((ROWS + HALO) // 8, 8, 128)
                    for group in range(taps_len // 8):
                        tap = wide_taps[pass_idx, taps_len - 1 - 8 * group - back, :, cols]
                        start = HALO // 8 - group
                        total = total + tap[None] * tiles[start : start + ROWS // 8]
                depthwise[:, cols] = total.reshape(ROWS, 128)
            hidden = normalise(depthwise[...])
            activated = (hidden * jax.nn.sigmoid(hidden)).astype(jnp.bfloat16)
            mask = row_mask(chunk)
            if chunk == chunks - 1:

                @pl.when(m == 0)
                def _():
                    weight_copies(pass_idx)[1].wait()

            rows = slice(chunk * ROWS, (chunk + 1) * ROWS)
            for block in range(feats // COLS):
                cols = slice(block * COLS, (block + 1) * COLS)
                added = slots[job, rows, cols].astype(jnp.float32) + jnp.dot(
                    activated, w2[pass_idx, :, cols], preferred_element_type=jnp.float32
                )
                outs[job, rows, cols] = jnp.where(mask, added, 0.0).astype(jnp.bfloat16)

            @pl.when(leaving)
            def _():
                for target in range(last):
                    exit_remote(m, chunk, target).start()
                exit_local(m, chunk).start()

            @pl.when(jnp.logical_not(leaving))
            def _():
                slot_copy(job, chunk).start()

        for chunk in reversed(range(chunks)):
            expand(chunk)
            if chunk < chunks - 1:
                finish(chunk + 1)

        @pl.when(tm > 0)
        def _():
            rim_copy(job).wait_recv()
            gated[0:HALO, :] = rims[job].astype(jnp.float32)

        @pl.when(tm == 0)
        def _():
            gated[0:HALO, :] = jnp.zeros((HALO, feats), jnp.float32)

        finish(0)
        return 0

    lax.fori_loop(0, jobs, run_job, 0)

    @pl.when(section != 0)
    def _():
        for m in range(micro):
            entry_remote(m, section).wait_send()

    def drain(job, _):
        leaving = jnp.logical_and(section == last, job >= jobs - micro)

        @pl.when(tm < tms - 1)
        def _():
            rim_copy(job).wait_send()

        for chunk in range(chunks):

            @pl.when(jnp.logical_not(leaving))
            def _():
                slot_copy(job, chunk).wait_send()

        return 0

    lax.fori_loop(0, jobs, drain, 0)

    @pl.when(section == last)
    def _():
        for m in range(micro):
            for chunk in range(chunks):
                for target in range(last):
                    exit_remote(m, chunk, target).wait_send()
                exit_local(m, chunk).wait()

    @pl.when(section != last)
    def _():
        for m in range(micro):
            for chunk in range(chunks):
                exit_remote(m, chunk, 0).wait_recv()


def per_device(inputs, lengths, w_expand, w_project, kernel, gain):
    sections = lax.axis_size("section")
    tms = lax.axis_size("tm")
    micro, frames, width = inputs.shape
    passes, _, feats, expanded = w_expand.shape
    taps = kernel.shape[2]
    chunks = frames // ROWS
    jobs = micro * passes
    hbm = pl.BlockSpec(memory_space=pl.ANY)
    dma = pltpu.SemaphoreType.DMA
    return pl.pallas_call(
        functools.partial(relay_kernel, sections, tms),
        out_shape=jax.ShapeDtypeStruct((micro, frames, width), jnp.bfloat16),
        in_specs=[pl.BlockSpec(memory_space=pltpu.SMEM)] + [hbm] * 5,
        out_specs=hbm,
        scratch_shapes=[
            pltpu.VMEM((passes, feats, expanded), jnp.bfloat16),
            pltpu.VMEM((passes, feats, feats), jnp.bfloat16),
            pltpu.VMEM((passes, taps, feats), jnp.float32),
            pltpu.VMEM((passes, 1, feats), jnp.float32),
            pltpu.VMEM((passes, taps, 8, feats), jnp.float32),
            pltpu.VMEM((jobs, frames, feats), jnp.bfloat16),
            pltpu.VMEM((jobs, frames, feats), jnp.bfloat16),
            pltpu.VMEM((jobs, HALO, feats), jnp.bfloat16),
            pltpu.VMEM((jobs, HALO, feats), jnp.bfloat16),
            pltpu.VMEM((HALO + frames, feats), jnp.float32),
            pltpu.VMEM((ROWS, feats), jnp.float32),
            dma((2, passes)),
            dma((2,)),
            dma((jobs, chunks)),
            dma((jobs, chunks)),
            dma((jobs,)),
            dma((jobs,)),
            dma((micro,)),
            dma((micro, sections)),
            dma((micro, chunks, sections)),
            dma((micro, chunks)),
        ],
        compiler_params=pltpu.CompilerParams(
            collective_id=0, has_side_effects=True, vmem_limit_bytes=40 << 20
        ),
        name="relay",
    )(
        lengths,
        inputs,
        w_expand.reshape(passes, feats, expanded),
        w_project.reshape(passes, feats, feats),
        kernel.reshape(passes, taps, feats),
        gain,
    )


def solution(mesh):
    in_specs = (
        P(None, "tm", "section"),
        P(),
        P(None, "section", None, None),
        P(None, "section", None, None),
        P(None, "section", None, None),
        P(None, "section", None),
    )
    out_specs = P(None, "tm", "section")
    return jax.shard_map(
        per_device, mesh=mesh, in_specs=in_specs, out_specs=out_specs, check_vma=False
    )
```

profile of v0, /device:TPU:192, one launch (start us, length us, event | category | flops | bytes accessed | tf_op | source)
XLA Modules:
  0.0 103.5 jit_solution(15171773645098197762)
XLA Ops:
  0.0 0.0 copy-start
  0.0 3.4 %copy-done = bf16[2,1,1024,2048]{3,2,1,0:T(8,128)(2,1)S(1)} copy-done((bf16[2,1,1024,2048]{3,2,1,0:T(8,128)(2,1)S(1)}, bf16[2,1,1024,2048]{3,2,1,0:T(8,128)(2,1)}, u32[]{:S(2)}) %copy-start) | copy-done | bytes 8388632
  3.4 0.0 copy-start.1
  3.4 2.2 %copy-done.1 = bf16[2,1,1024,1024]{3,2,1,0:T(8,128)(2,1)S(1)} copy-done((bf16[2,1,1024,1024]{3,2,1,0:T(8,128)(2,1)S(1)}, bf16[2,1,1024,1024]{3,2,1,0:T(8,128)(2,1)}, u32[]{:S(2)}) %copy-start.1) | copy-done | bytes 4194328
  5.6 0.0 copy-start.2
  5.6 0.9 copy-done.2
  6.5 0.0 copy-start.3
  6.5 0.9 copy-done.3
  7.4 0.0 copy-start.4
  7.5 0.7 copy-done.4
  8.1 0.0 copy-start.5
  8.1 0.7 copy-done.5
  8.8 94.1 %relay.1 = bf16[3,128,256]{2,1,0:T(8,128)(2,1)S(1)} custom-call(s32[3]{0:T(128)S(1)} %copy-done.5, bf16[3,128,256]{2,1,0:T(8,128)(2,1)S(1)} %copy-done.3, bf16[2,1024,2048]{2,1,0:T(8,128)(2,1)S(1)} %bitcast.3, bf16[2,1024,1024]{2,1,0:T(8,128)(2,1)S(1)} %bitcast.4, f32[2,32,1024]{2,1,0:T(8,128)S(1)} %bitcast.5, f32[2,1,1024]{2,1,0:T(1,128)S(1)} %copy-done.4), custom_call_target="tpu_custom_call" | custom-call | tf_op jit(solution)/shard_map/relay/pallas_call | solution.py:337
  102.9 0.7 copy.8
Async XLA Ops:
  0.0 3.4 %copy-start = (bf16[2,1,1024,2048]{3,2,1,0:T(8,128)(2,1)S(1)}, bf16[2,1,1024,2048]{3,2,1,0:T(8,128)(2,1)}, u32[]{:S(2)}) copy-start(bf16[2,1,1024,2048]{3,2,1,0:T(8,128)(2,1)} %param.8) | copy-start | bytes 25165828
  3.4 2.2 %copy-start.1 = (bf16[2,1,1024,1024]{3,2,1,0:T(8,128)(2,1)S(1)}, bf16[2,1,1024,1024]{3,2,1,0:T(8,128)(2,1)}, u32[]{:S(2)}) copy-start(bf16[2,1,1024,1024]{3,2,1,0:T(8,128)(2,1)} %param.9) | copy-start | bytes 12582916
  5.6 0.9 copy-start.2
  6.5 0.9 copy-start.3
  7.4 0.7 copy-start.4
  8.1 0.7 copy-start.5
where the time goes:
time: 104 us
  Pallas kernels  94.1 us (90%)
  local copies, waits for them, and re-layouts  9.47 us (9%)
    pallas_call x1, Pallas kernels, per_device(): pl.pallas_call(functools.partial(relay_kernel, sections, tms), out_shape=...  94.1 us
    unnamed x13, local copies, waits for them, and re-layouts  9.47 us

commit v1 on v0

--- a/solution.py
+++ b/solution.py
@@ -92,30 +92,36 @@
     greeted = sections - 1 + (tm > 0).astype(jnp.int32) + (tm < tms - 1).astype(jnp.int32)
     pl.semaphore_wait(barrier, greeted)
 
-    def entry_remote(m, source):
-        return pltpu.make_async_remote_copy(
-            src_ref=inputs_hbm.at[m],
-            dst_ref=slots.at[m, :, pl.ds(pl.multiple_of(source * width, width), width)],
-            send_sem=entry_send.at[m],
-            recv_sem=entry_recv.at[m, source],
+    def entry_remote(m, chunk, source):
+        rows = pl.ds(chunk * ROWS, ROWS)
+        return pltpu.make_async_remote_copy(
+            src_ref=inputs_hbm.at[m, rows],
+            dst_ref=slots.at[m, rows, pl.ds(pl.multiple_of(source * width, width), width)],
+            send_sem=entry_send.at[m, chunk],
+            recv_sem=entry_recv.at[m, chunk, source],
             device_id={"section": 0},
             device_id_type=MESH,
         )
 
-    def entry_local(m):
+    def entry_local(m, chunk):
+        rows = pl.ds(chunk * ROWS, ROWS)
         return pltpu.make_async_copy(
-            inputs_hbm.at[m], slots.at[m, :, pl.ds(0, width)], entry_recv.at[m, 0]
+            inputs_hbm.at[m, rows], slots.at[m, rows, pl.ds(0, width)], entry_recv.at[m, chunk, 0]
         )
 
     @pl.when(section == 0)
     def _():
         for m in range(micro):
-            entry_local(m).start()
+            for chunk in reversed(range(chunks)):
+                entry_local(m, chunk).start()
 
     @pl.when(section != 0)
     def _():
         for m in range(micro):
-            entry_remote(m, section).start()
+            for chunk in reversed(range(chunks)):
+                entry_remote(m, chunk, section).start()
+            for chunk in reversed(range(chunks)):
+                entry_remote(m, chunk, section).wait_send()
 
     taps_copy.wait()
     gain_copy.wait()
@@ -186,13 +192,13 @@
             rows = lax.broadcasted_iota(jnp.int32, (ROWS, 1), 0) + (tm * frames + chunk * ROWS)
             return rows < length
 
-        @pl.when(first)
-        def _():
-            entry_local(m).wait()
-            for source in range(1, sections):
-                entry_remote(m, source).wait_recv()
-
         def expand(chunk):
+            @pl.when(first)
+            def _():
+                entry_local(m, chunk).wait()
+                for source in range(1, sections):
+                    entry_remote(m, chunk, source).wait_recv()
+
             @pl.when(jnp.logical_not(first))
             def _():
                 slot_arrival(job, chunk).wait_recv()
@@ -287,10 +293,6 @@
 
     lax.fori_loop(0, jobs, run_job, 0)
 
-    @pl.when(section != 0)
-    def _():
-        for m in range(micro):
-            entry_remote(m, section).wait_send()
 
     def drain(job, _):
         leaving = jnp.logical_and(section == last, job >= jobs - micro)
@@ -332,7 +334,7 @@
     taps = kernel.shape[2]
     chunks = frames // ROWS
     jobs = micro * passes
-    hbm = pl.BlockSpec(memory_space=pl.ANY)
+    hbm = pl.BlockSpec(memory_space=pltpu.HBM)
     dma = pltpu.SemaphoreType.DMA
     return pl.pallas_call(
         functools.partial(relay_kernel, sections, tms),
@@ -357,13 +359,13 @@
             dma((jobs, chunks)),
             dma((jobs,)),
             dma((jobs,)),
-            dma((micro,)),
-            dma((micro, sections)),
+            dma((micro, chunks)),
+            dma((micro, chunks, sections)),
             dma((micro, chunks, sections)),
             dma((micro, chunks)),
         ],
         compiler_params=pltpu.CompilerParams(
-            collective_id=0, has_side_effects=True, vmem_limit_bytes=40 << 20
+            collective_id=0, has_side_effects=True, vmem_limit_bytes=63 << 20
         ),
         name="relay",
     )(

time: 104 us -> 93.1 us (0.90)
  local copies, waits for them, and re-layouts: 9.47 us -> 1.62 us
  Pallas kernels: 94.1 us -> 90.9 us
    unnamed x13 -> x1, local copies, waits for them, and re-layouts: 9.47 us -> 1.62 us
    pallas_call x1, Pallas kernels: 94.1 us -> 90.9 us  [per_device(): pl.pallas_call(functools.partial(relay_kernel, sections, tms), out_shape=...]
where the time goes in v1:
time: 93.1 us; the launch traced here: 92.5 us
  Pallas kernels  90.9 us (98%)
  local copies, waits for them, and re-layouts  1.62 us (2%)
    pallas_call x1, Pallas kernels, per_device(): pl.pallas_call(functools.partial(relay_kernel, sections, tms), out_shape=...  90.9 us

profile of v1, /device:TPU:192, one launch (start us, length us, event | category | flops | bytes accessed | tf_op | source)
XLA Modules:
  0.0 92.5 jit_solution(7882643091875002688)
XLA Ops:
  0.0 90.9 %relay.1 = bf16[3,128,256]{2,1,0:T(8,128)(2,1)} custom-call(s32[3]{0:T(128)} %lengths_ref.1, bf16[3,128,256]{2,1,0:T(8,128)(2,1)} %inputs_hbm.1, bf16[2,1024,2048]{2,1,0:T(8,128)(2,1)} %bitcast.3, bf16[2,1024,1024]{2,1,0:T(8,128)(2,1)} %bitcast.4, f32[2,32,1024]{2,1,0:T(8,128)} %bitcast.5, f32[2,1,1024]{2,1,0:T(1,128)} %gain_hbm.1), custom_call_target="tpu_custom_call" | custom-call | tf_op jit(solution)/shard_map/relay/pallas_call | solution.py:339
  90.9 1.6 %copy.8 = bf16[3,128,256]{2,1,0:T(8,128)(2,1)} copy(bf16[3,128,256]{2,1,0:T(8,128)(2,1)} %relay.1) | data formatting | bytes 393216

commit v2 on v1

--- a/solution.py
+++ b/solution.py
@@ -11,6 +11,15 @@
 ROWS = 32
 HALO = 32
 COLS = 256
+PLAN = (
+    ("expand", 3, 2),
+    ("finish", 3, 3),
+    ("expand", 1, 1),
+    ("finish", 2, 2),
+    ("expand", 0, 0),
+    ("finish", 1, 1),
+    ("finish", 0, 0),
+)
 
 
 def normalise(values):
@@ -188,11 +197,12 @@
         first = jnp.logical_and(section == 0, pass_idx == 0)
         leaving = jnp.logical_and(section == last, pass_idx == passes - 1)
 
-        def row_mask(chunk):
-            rows = lax.broadcasted_iota(jnp.int32, (ROWS, 1), 0) + (tm * frames + chunk * ROWS)
+        def row_mask(low, high):
+            count = (high + 1 - low) * ROWS
+            rows = lax.broadcasted_iota(jnp.int32, (count, 1), 0) + (tm * frames + low * ROWS)
             return rows < length
 
-        def expand(chunk):
+        def arrive(chunk):
             @pl.when(first)
             def _():
                 entry_local(m, chunk).wait()
@@ -203,92 +213,95 @@
             def _():
                 slot_arrival(job, chunk).wait_recv()
 
-            if chunk == chunks - 1:
+        def expand(high, low):
+            for chunk in reversed(range(low, high + 1)):
+                arrive(chunk)
+            opening = high == chunks - 1
+            if opening:
 
                 @pl.when(m == 0)
                 def _():
                     weight_copies(pass_idx)[0].wait()
 
-            values = slots[job, chunk * ROWS : (chunk + 1) * ROWS, :].astype(jnp.float32)
+            top, end = low * ROWS, (high + 1) * ROWS
+            values = slots[job, top:end, :].astype(jnp.float32)
             normed = (normalise(values) * gain[pass_idx]).astype(jnp.bfloat16)
-            mask = row_mask(chunk)
+            mask = row_mask(low, high)
             for block in range(feats // COLS):
-                low = block * COLS
-                value = jnp.dot(
-                    normed, w1[pass_idx, :, low : low + COLS], preferred_element_type=jnp.float32
-                )
+                left = block * COLS
+                cols = slice(left, left + COLS)
+                value = jnp.dot(normed, w1[pass_idx, :, cols], preferred_element_type=jnp.float32)
                 gate = jnp.dot(
                     normed,
-                    w1[pass_idx, :, feats + low : feats + low + COLS],
+                    w1[pass_idx, :, feats + left : feats + left + COLS],
                     preferred_element_type=jnp.float32,
                 )
-                passed = jnp.where(mask, value * jax.nn.sigmoid(gate), 0.0).astype(jnp.bfloat16)
-                gated[HALO + chunk * ROWS : HALO + (chunk + 1) * ROWS, low : low + COLS] = (
-                    passed.astype(jnp.float32)
-                )
-                if chunk == chunks - 1:
-                    tails[job, :, low : low + COLS] = passed[ROWS - HALO :, :]
-            if chunk == chunks - 1:
+                passed = jnp.where(mask, value * jax.nn.sigmoid(gate), 0.0)
+                gated[HALO + top : HALO + end, cols] = passed
+                if opening:
+                    tails[job, :, cols] = passed[end - top - HALO :, :].astype(jnp.bfloat16)
+            if opening:
 
                 @pl.when(tm < tms - 1)
                 def _():
                     rim_copy(job).start()
 
-        def finish(chunk):
+        def finish(high, low):
+            if low == 0:
+
+                @pl.when(tm > 0)
+                def _():
+                    rim_copy(job).wait_recv()
+                    gated[0:HALO, :] = rims[job].astype(jnp.float32)
+
+                @pl.when(tm == 0)
+                def _():
+                    gated[0:HALO, :] = jnp.zeros((HALO, feats), jnp.float32)
+
+            top, end = low * ROWS, (high + 1) * ROWS
+            count = end - top
             for block in range(feats // 128):
                 cols = slice(block * 128, (block + 1) * 128)
-                window = gated[chunk * ROWS : (chunk + 1) * ROWS + HALO, cols]
-                total = jnp.zeros((ROWS // 8, 8, 128), jnp.float32)
+                window = gated[top : end + HALO, cols]
+                total = jnp.zeros((count // 8, 8, 128), jnp.float32)
                 for back in range(8):
                     moved = window if back == 0 else pltpu.roll(window, back, 0)
-                    tiles = moved.reshape((ROWS + HALO) // 8, 8, 128)
+                    tiles = moved.reshape((count + HALO) // 8, 8, 128)
                     for group in range(taps_len // 8):
                         tap = wide_taps[pass_idx, taps_len - 1 - 8 * group - back, :, cols]
                         start = HALO // 8 - group
-                        total = total + tap[None] * tiles[start : start + ROWS // 8]
-                depthwise[:, cols] = total.reshape(ROWS, 128)
-            hidden = normalise(depthwise[...])
+                        total = total + tap[None] * tiles[start : start + count // 8]
+                depthwise[0:count, cols] = total.reshape(count, 128)
+            hidden = normalise(depthwise[0:count, :])
             activated = (hidden * jax.nn.sigmoid(hidden)).astype(jnp.bfloat16)
-            mask = row_mask(chunk)
-            if chunk == chunks - 1:
+            mask = row_mask(low, high)
+            if high == chunks - 1:
 
                 @pl.when(m == 0)
                 def _():
                     weight_copies(pass_idx)[1].wait()
 
-            rows = slice(chunk * ROWS, (chunk + 1) * ROWS)
             for block in range(feats // COLS):
                 cols = slice(block * COLS, (block + 1) * COLS)
-                added = slots[job, rows, cols].astype(jnp.float32) + jnp.dot(
+                added = slots[job, top:end, cols].astype(jnp.float32) + jnp.dot(
                     activated, w2[pass_idx, :, cols], preferred_element_type=jnp.float32
                 )
-                outs[job, rows, cols] = jnp.where(mask, added, 0.0).astype(jnp.bfloat16)
+                outs[job, top:end, cols] = jnp.where(mask, added, 0.0).astype(jnp.bfloat16)
 
             @pl.when(leaving)
             def _():
-                for target in range(last):
-                    exit_remote(m, chunk, target).start()
-                exit_local(m, chunk).start()
+                for chunk in reversed(range(low, high + 1)):
+                    for target in range(last):
+                        exit_remote(m, chunk, target).start()
+                    exit_local(m, chunk).start()
 
             @pl.when(jnp.logical_not(leaving))
             def _():
-                slot_copy(job, chunk).start()
-
-        for chunk in reversed(range(chunks)):
-            expand(chunk)
-            if chunk < chunks - 1:
-                finish(chunk + 1)
-
-        @pl.when(tm > 0)
-        def _():
-            rim_copy(job).wait_recv()
-            gated[0:HALO, :] = rims[job].astype(jnp.float32)
-
-        @pl.when(tm == 0)
-        def _():
-            gated[0:HALO, :] = jnp.zeros((HALO, feats), jnp.float32)
-
-        finish(0)
+                for chunk in reversed(range(low, high + 1)):
+                    slot_copy(job, chunk).start()
+
+        for act, high, low in PLAN:
+            (expand if act == "expand" else finish)(high, low)
         return 0
 
     lax.fori_loop(0, jobs, run_job, 0)
@@ -352,7 +365,7 @@
             pltpu.VMEM((jobs, HALO, feats), jnp.bfloat16),
             pltpu.VMEM((jobs, HALO, feats), jnp.bfloat16),
             pltpu.VMEM((HALO + frames, feats), jnp.float32),
-            pltpu.VMEM((ROWS, feats), jnp.float32),
+            pltpu.VMEM((frames, feats), jnp.float32),
             dma((2, passes)),
             dma((2,)),
             dma((jobs, chunks)),

time: 93.1 us -> 92.9 us (level)
  no operation moved by 1% of the time
where the time goes in v2:
time: 92.9 us; the launch traced here: 92.7 us
  Pallas kernels  91.1 us (98%)
  local copies, waits for them, and re-layouts  1.62 us (2%)
    pallas_call x1, Pallas kernels, per_device(): pl.pallas_call(functools.partial(relay_kernel, sections, tms), out_shape=...  91.1 us

profile of v2, /device:TPU:192, one launch (start us, length us, event | category | flops | bytes accessed | tf_op | source)
XLA Modules:
  0.0 92.7 jit_solution(8136182641765391089)
XLA Ops:
  0.0 91.1 %relay.1 = bf16[3,128,256]{2,1,0:T(8,128)(2,1)} custom-call(s32[3]{0:T(128)} %lengths_ref.1, bf16[3,128,256]{2,1,0:T(8,128)(2,1)} %inputs_hbm.1, bf16[2,1024,2048]{2,1,0:T(8,128)(2,1)} %bitcast.3, bf16[2,1024,1024]{2,1,0:T(8,128)(2,1)} %bitcast.4, f32[2,32,1024]{2,1,0:T(8,128)} %bitcast.5, f32[2,1,1024]{2,1,0:T(1,128)} %gain_hbm.1), custom_call_target="tpu_custom_call" | custom-call | tf_op jit(solution)/shard_map/relay/pallas_call | solution.py:352
  91.1 1.6 %copy.8 = bf16[3,128,256]{2,1,0:T(8,128)(2,1)} copy(bf16[3,128,256]{2,1,0:T(8,128)(2,1)} %relay.1) | data formatting | bytes 393216
